TPU v7x, 32 devices: a whole 2x2x4 slice. The times are simulated.
32 devices in a mesh: groups: 2 (over y), phi: 4 (over z), ev: 4 (over x, core).
Axes of the slice: x: 2, y: 2, z: 4, core: 2. Of those that a mesh axis runs over, the one named last changes fastest.
Arguments:
- cell_feats: bfloat16 [8, 1024, 256], P(('groups', 'ev'), 'phi'), parts along dimension 0, may hold values from -3 to 3
- neighbours: int32 [8, 8, 4], P(('groups', 'ev'), 'phi'), parts along dimension 0, may hold values from 0 to 3
- member_cell: int32 [8, 512], P(('groups', 'ev'), 'phi'), parts along dimension 0, may hold values from 0 to 255, as said below
- member_jet: int32 [8, 512, 1], P(('groups', 'ev'), 'phi'), parts along dimension 0, may hold values from 0 to 15, as said below
- cotangent: bfloat16 [8, 1024, 256], P(('groups', 'ev'), 'phi'), parts along dimension 0, may hold values from -3 to 3
- message_weight: bfloat16 [256, 256], replicated, may hold values from -0.375 to 0.375
- query_weight: bfloat16 [256, 256], replicated, may hold values from -4 to 4
- key_weight: bfloat16 [256, 256], replicated, may hold values from -4 to 4
- value_weight: bfloat16 [256, 256], replicated, may hold values from -0.375 to 0.375
- output_weight: bfloat16 [256, 256], replicated, may hold values from -0.375 to 0.375
Outputs:
- out_cells: bfloat16 [8, 1024, 256], P(('groups', 'ev'), 'phi'), parts along dimension 0
- grad_cells: bfloat16 [8, 1024, 256], P(('groups', 'ev'), 'phi'), parts along dimension 0
- grad_message: float32 [512, 256], P('groups'), parts along dimension 0
- grad_query: float32 [512, 256], P('groups'), parts along dimension 0
- grad_key: float32 [512, 256], P('groups'), parts along dimension 0
- grad_value: float32 [512, 256], P('groups'), parts along dimension 0
- grad_output: float32 [512, 256], P('groups'), parts along dimension 0
There are 2 independent parts, one for each index of `groups`. A program takes and returns all parts, laid end to end along the dimension named above; an argument that names none is the same for every part. Nothing has to cross between parts.
Inputs may be any that keep to these rules, and one draw needn't show every extreme that they name: `member_cell`: within one sector's 128 constituents of an event the cells are distinct. `member_jet`: A constituent of sector p belongs to a jet owned by one of the sectors p - 1 to p + 1 on the loop (jet j is owned by sector j // 4). Among one sector's 128 constituents of an event at most 21 belong to one jet, and some jet has exactly 21 of them.
All inputs are finite; a program needn't handle non-finite values.
Results may differ from a plain program's by a relative error of at most 0.0065.
The roundings to bfloat16 on the way count: a program that leaves them out, or rounds other values in their place, can miss the bound.
Values may be sent and summed in bfloat16 or wider, within the bound.
No kernel may reach another device: no remote copies, remote signals or barrier semaphores. Data moves between devices by JAX's collectives and lax.ppermute only.
A program may use at most 64 MiB of HBM per device.

v0:
```python
import math
import jax
import jax.numpy as jnp
from jax import lax
from jax.sharding import PartitionSpec as P

HEADS = 8
BLOCK = 128
NBRS = 4
JET_DEV = 4


def extended_2(cells, sides, width):
    for axis, dim in sides:
        count = lax.axis_size(axis)
        head = lax.slice_in_dim(cells, 0, width, axis=dim)
        tail = lax.slice_in_dim(cells, cells.shape[dim] - width, cells.shape[dim], axis=dim)
        cells = jnp.concatenate(
            [
                lax.ppermute(tail, axis, [(i, (i + 1) % count) for i in range(count)]),
                cells,
                lax.ppermute(head, axis, [((i + 1) % count, i) for i in range(count)]),
            ],
            axis=dim,
        )
    return cells


def shortened(value):
    return jax.tree.map(lambda a: a.astype(jnp.bfloat16) if a.dtype == jnp.float32 else a, value)


def passed_along(block, axis, distance):
    devices = range(lax.axis_size(axis))
    route = [((i - distance) % len(devices), i) for i in devices]
    return lax.ppermute(block, axis, route)


def silu_slope(values):
    sigmoid = jax.nn.sigmoid(values)
    return sigmoid * (1.0 + values * (1.0 - sigmoid))


def attend_forward(members, present, query_weight, key_weight, value_weight, output_weight):
    jet_count, slot_count, channels = members.shape
    head_size = channels // HEADS
    score_scale = 1.0 / math.sqrt(head_size)
    flat_members = members.reshape(jet_count * slot_count, channels)

    def project(weight):
        result = jnp.dot(flat_members, weight, preferred_element_type=jnp.float32)
        return result.astype(jnp.bfloat16).reshape(jet_count, slot_count, HEADS, head_size)

    queries = project(query_weight)
    keyed = project(key_weight)
    valued = project(value_weight)
    scores = jnp.einsum("jqnd,jknd->jnqk", queries, keyed, preferred_element_type=jnp.float32)
    scores = jnp.where(present[:, None, None, :] > 0.5, scores * score_scale, -1e30)
    largest = jnp.max(scores, axis=-1, keepdims=True)
    powers = jnp.exp(scores - largest)
    chances = powers / jnp.sum(powers, axis=-1, keepdims=True)
    chances_low = chances.astype(jnp.bfloat16)
    mixture = jnp.einsum("jnqk,jknd->jqnd", chances_low, valued, preferred_element_type=jnp.float32)
    mixture = mixture.astype(jnp.bfloat16).reshape(jet_count * slot_count, channels)
    attended = jnp.dot(mixture, output_weight, preferred_element_type=jnp.float32).astype(
        jnp.bfloat16
    )
    return (
        attended.reshape(jet_count, slot_count, channels),
        (queries, keyed, valued, chances, chances_low, mixture),
    )


def attend_backward(
    members, saved, upstream, query_weight, key_weight, value_weight, output_weight
):
    queries, keyed, valued, chances, chances_low, mixture = saved
    jet_count, slot_count, channels = members.shape
    head_size = channels // HEADS
    score_scale = 1.0 / math.sqrt(head_size)
    flat_members = members.reshape(jet_count * slot_count, channels)
    flat_upstream = upstream.reshape(jet_count * slot_count, channels)
    output_term = jnp.dot(mixture.T, flat_upstream, preferred_element_type=jnp.float32)
    grad_mix = jnp.dot(flat_upstream, output_weight.T, preferred_element_type=jnp.float32)
    grad_mix = grad_mix.astype(jnp.bfloat16).reshape(jet_count, slot_count, HEADS, head_size)
    grad_chances = jnp.einsum(
        "jqnd,jknd->jnqk", grad_mix, valued, preferred_element_type=jnp.float32
    )
    grad_vals = jnp.einsum(
        "jnqk,jqnd->jknd", chances_low, grad_mix, preferred_element_type=jnp.float32
    )
    grad_vals = grad_vals.astype(jnp.bfloat16)
    inner_sum = jnp.sum(chances * grad_chances, axis=-1, keepdims=True)
    grad_scores = (chances * (grad_chances - inner_sum) * score_scale).astype(jnp.bfloat16)
    grad_queries = jnp.einsum(
        "jnqk,jknd->jqnd", grad_scores, keyed, preferred_element_type=jnp.float32
    )
    grad_keys = jnp.einsum(
        "jnqk,jqnd->jknd", grad_scores, queries, preferred_element_type=jnp.float32
    )
    flat_queries = grad_queries.astype(jnp.bfloat16).reshape(jet_count * slot_count, channels)
    flat_keys = grad_keys.astype(jnp.bfloat16).reshape(jet_count * slot_count, channels)
    flat_vals = grad_vals.reshape(jet_count * slot_count, channels)
    query_term = jnp.dot(flat_members.T, flat_queries, preferred_element_type=jnp.float32)
    key_term = jnp.dot(flat_members.T, flat_keys, preferred_element_type=jnp.float32)
    value_term = jnp.dot(flat_members.T, flat_vals, preferred_element_type=jnp.float32)
    grad_members = jnp.dot(flat_queries, query_weight.T, preferred_element_type=jnp.float32)
    grad_members = grad_members + jnp.dot(
        flat_keys, key_weight.T, preferred_element_type=jnp.float32
    )
    grad_members = grad_members + jnp.dot(
        flat_vals, value_weight.T, preferred_element_type=jnp.float32
    )
    grad_members = grad_members.astype(jnp.bfloat16).reshape(jet_count, slot_count, channels)
    return (grad_members, (query_term, key_term, value_term, output_term))


def direct_route(entries, mover):
    radius = (len(entries) - 1) // 2
    routed = []
    for slot_index in range(len(entries)):
        if slot_index == radius:
            routed.append(entries[radius])
        else:
            routed.append(mover(entries[2 * radius - slot_index], radius - slot_index))
    return routed


def on_device(
    cell_feats,
    neighbours,
    member_cell,
    member_jet,
    cotangent,
    message_weight,
    query_weight,
    key_weight,
    value_weight,
    output_weight,
):
    events, per_device, channels = cell_feats.shape
    sectors = lax.axis_size("phi")
    sector = lax.axis_index("phi")
    blocks = per_device // BLOCK
    members_dev = member_cell.shape[1]
    radius = min(4, (sectors - 1) // 2)
    window = 2 * radius + 1
    capacity = max(2, 2 * members_dev // (JET_DEV * window))
    slot_count = window * capacity
    window_jets = window * JET_DEV
    tiles = cell_feats.reshape(events, blocks, BLOCK, channels)
    extended = extended_2(tiles, (("phi", 1),), 1)
    counts = jnp.sum(
        (neighbours[..., None] == jnp.arange(blocks + 2, dtype=jnp.int32)).astype(jnp.bfloat16),
        axis=2,
    )
    gathered = jnp.einsum(
        "ebj,ejch->ebch", counts, extended, preferred_element_type=jnp.float32
    ) * (1.0 / NBRS)
    flat_gathered = gathered.astype(jnp.bfloat16).reshape(events * per_device, channels)
    before_act = jnp.dot(flat_gathered, message_weight, preferred_element_type=jnp.float32)
    hidden = (
        cell_feats.reshape(-1, channels).astype(jnp.float32) + jax.nn.silu(before_act)
    ).astype(jnp.bfloat16)
    hidden = hidden.reshape(events, per_device, channels)
    jet_ids = member_jet[..., 0]
    owner = jet_ids // JET_DEV
    offset_slot = (owner - sector + radius + sectors) % sectors
    local_ids = offset_slot * JET_DEV + jet_ids % JET_DEV
    positions = jnp.arange(members_dev, dtype=jnp.int32)
    jet_match = local_ids[..., None] == jnp.arange(window_jets, dtype=jnp.int32)
    earlier = (positions[:, None] > positions[None, :]).astype(jnp.bfloat16)
    prior = jnp.einsum(
        "ik,ekj->eij", earlier, jet_match.astype(jnp.bfloat16), preferred_element_type=jnp.float32
    )
    ranks = jnp.sum(jnp.where(jet_match, prior, 0.0), axis=-1).astype(jnp.int32)
    targets = local_ids * capacity + ranks
    slot_ids = jnp.arange(window_jets * capacity, dtype=jnp.int32)
    occupant = (
        jnp.sum(jnp.where(targets[..., None] == slot_ids, positions[None, :, None] + 1, 0), axis=1)
        - 1
    )
    picked = jnp.where(occupant >= 0, occupant, members_dev)
    cell_ids = jnp.arange(per_device, dtype=jnp.int32)
    holder = (
        jnp.sum(
            jnp.where(member_cell[..., None] == cell_ids, positions[None, :, None] + 1, 0), axis=1
        )
        - 1
    )
    holder_pick = jnp.where(holder >= 0, holder, members_dev)

    def to_slots(source):
        chosen = jnp.take_along_axis(source, member_cell[..., None], axis=1)
        padded = jnp.concatenate([chosen, jnp.zeros((events, 1, channels), chosen.dtype)], axis=1)
        placed_rows = jnp.take_along_axis(padded, picked[..., None], axis=1)
        return placed_rows.reshape(events, window, JET_DEV, capacity, channels)

    def to_cells(arrived_rows):
        flattened = arrived_rows.reshape(events, window_jets * capacity, channels)
        returned = jnp.take_along_axis(flattened, targets[..., None], axis=1)
        padded = jnp.concatenate(
            [returned, jnp.zeros((events, 1, channels), returned.dtype)], axis=1
        )
        return jnp.take_along_axis(padded, holder_pick[..., None], axis=1)

    feature_slots = to_slots(hidden)
    grad_slots = to_slots(cotangent)
    mask_slots = (occupant >= 0).astype(jnp.bfloat16).reshape(events, window, JET_DEV, capacity)
    outgoing = [
        (feature_slots[:, slot_index], grad_slots[:, slot_index], mask_slots[:, slot_index])
        for slot_index in range(window)
    ]
    arrived = direct_route(
        outgoing,
        lambda bundle, distance: jax.tree.map(
            lambda part, own: part.astype(own.dtype),
            passed_along(shortened(bundle), "phi", distance),
            bundle,
        ),
    )
    members = jnp.stack([entry[0] for entry in arrived], axis=2).reshape(
        events * JET_DEV, slot_count, channels
    )
    upstream = jnp.stack([entry[1] for entry in arrived], axis=2).reshape(
        events * JET_DEV, slot_count, channels
    )
    present = jnp.stack([entry[2] for entry in arrived], axis=2).reshape(
        events * JET_DEV, slot_count
    )
    attended, saved = attend_forward(
        members, present, query_weight, key_weight, value_weight, output_weight
    )
    grad_members, weight_terms = attend_backward(
        members, saved, upstream, query_weight, key_weight, value_weight, output_weight
    )
    attended_view = attended.reshape(events, JET_DEV, window, capacity, channels)
    grad_view = grad_members.reshape(events, JET_DEV, window, capacity, channels)
    returning = [
        (attended_view[:, :, slot_index], grad_view[:, :, slot_index])
        for slot_index in range(window)
    ]
    delivered = direct_route(
        returning,
        lambda bundle, distance: jax.tree.map(
            lambda part, own: part.astype(own.dtype),
            passed_along(shortened(bundle), "phi", distance),
            bundle,
        ),
    )
    returned_out = jnp.stack([entry[0] for entry in delivered], axis=1)
    returned_grad = jnp.stack([entry[1] for entry in delivered], axis=1)
    out_cells = (hidden.astype(jnp.float32) + to_cells(returned_out).astype(jnp.float32)).astype(
        jnp.bfloat16
    )
    grad_hidden = cotangent.astype(jnp.float32) + to_cells(returned_grad).astype(jnp.float32)
    grad_before = (grad_hidden.reshape(-1, channels) * silu_slope(before_act)).astype(jnp.bfloat16)
    message_term = jnp.dot(flat_gathered.T, grad_before, preferred_element_type=jnp.float32)
    grad_gathered = jnp.dot(
        grad_before, message_weight.T, preferred_element_type=jnp.float32
    ).astype(jnp.bfloat16)
    grad_gathered = grad_gathered.reshape(events, blocks, BLOCK, channels)
    grad_extended = jnp.einsum(
        "ebj,ebch->ejch", counts, grad_gathered, preferred_element_type=jnp.float32
    ) * (1.0 / NBRS)
    grad_extended = grad_extended.astype(jnp.bfloat16)
    from_lower = passed_along(grad_extended[:, blocks + 1 :], "phi", 1)
    from_upper = passed_along(grad_extended[:, :1], "phi", -1)
    summed = grad_hidden.reshape(events, blocks, BLOCK, channels) + grad_extended[
        :, 1 : blocks + 1
    ].astype(jnp.float32)
    summed = summed + jnp.pad(
        from_lower.astype(jnp.float32), ((0, 0), (0, blocks - 1), (0, 0), (0, 0))
    )
    summed = summed + jnp.pad(
        from_upper.astype(jnp.float32), ((0, 0), (blocks - 1, 0), (0, 0), (0, 0))
    )
    grad_cells = summed.astype(jnp.bfloat16).reshape(events, per_device, channels)
    totals = lax.psum(
        (message_term, weight_terms[0], weight_terms[1], weight_terms[2], weight_terms[3]),
        ("phi", "ev"),
    )
    squares = jnp.sum(jnp.stack([jnp.sum(matrix * matrix) for matrix in totals]))
    bound = math.sqrt(5.0) * channels
    factor = bound / jnp.maximum(jnp.sqrt(squares), bound)
    return (
        out_cells,
        grad_cells,
        totals[0] * factor,
        totals[1] * factor,
        totals[2] * factor,
        totals[3] * factor,
        totals[4] * factor,
    )


def solution(mesh):
    in_specs = (
        P(("groups", "ev"), "phi", None),
        P(("groups", "ev"), "phi", None),
        P(("groups", "ev"), "phi"),
        P(("groups", "ev"), "phi", None),
        P(("groups", "ev"), "phi", None),
        P(),
        P(),
        P(),
        P(),
        P(),
    )
    out_specs = (
        P(("groups", "ev"), "phi", None),
        P(("groups", "ev"), "phi", None),
        P("groups", None),
        P("groups", None),
        P("groups", None),
        P("groups", None),
        P("groups", None),
    )
    return jax.shard_map(
        on_device, mesh=mesh, in_specs=in_specs, out_specs=out_specs, check_vma=False
    )
```

profile of v0, /device:TPU:0, one launch (start us, length us, event | category | flops | bytes accessed | tf_op | source)
XLA Modules:
  0.0 195.5 jit_solution(7533739546687173720)
XLA Ops:
  8.2 4.6 %fusion.41 = s32[252]{0:T(256)S(1)} fusion(s32[128]{0:T(128)S(1)} %iota_add_fusion, s32[128]{0:T(128)S(1)} %get-tuple-element.42), kind=kLoop, calls=%fused_computation.93 | loop fusion | flops 96516 | bytes 2032 | tf_op jit(solution)/shard_map/reduce_sum | solution.py:180
  12.9 3.1 %collective-permute-start.4 = (bf16[1,4,21]{2,1,0:T(4,128)(2,1)S(1)}, bf16[1,4,21]{2,1,0:T(4,128)(2,1)S(1)}, u32[]{:S(2)}, u32[]{:S(2)}) collective-permute-start(bf16[1,4,21]{2,1,0:T(4,128)(2,1)S(1)} %get-tuple-element.38), channel_id=1, source_target_pairs={{12,0},{0,4},{4,8},{8,12},{13,1},{1,5},{5,9},{9,13},{14,2},{2,6},{... | collective-permute-start | bytes 512 | tf_op jit(solution)/shard_map/ppermute | solution.py:36
  16.0 2.1 %collective-permute-start.5 = (bf16[1,4,21]{2,1,0:T(4,128)(2,1)S(1)}, bf16[1,4,21]{2,1,0:T(4,128)(2,1)S(1)}, u32[]{:S(2)}, u32[]{:S(2)}) collective-permute-start(bf16[1,4,21]{2,1,0:T(4,128)(2,1)S(1)} %get-tuple-element.39), channel_id=1, source_target_pairs={{4,0},{8,4},{12,8},{0,12},{5,1},{9,5},{13,9},{1,13},{6,2},{10,6},{... | collective-permute-start | bytes 512 | tf_op jit(solution)/shard_map/ppermute | solution.py:36
  18.1 1.0 copy.103
  19.4 3.8 %collective-permute-start.1 = (bf16[1,1,128,256]{3,1,2,0:T(2,128)(2,1)S(1)}, bf16[1,1,128,256]{3,1,2,0:T(2,128)(2,1)S(1)}, u32[]{:S(2)}, u32[]{:S(2)}) collective-permute-start(bf16[1,1,128,256]{3,1,2,0:T(2,128)(2,1)S(1)} %get-tuple-element.37), channel_id=1, source_target_pairs={{4,0},{8,4},{12,8},{0,12},{5,1},{9,5},{13,9},{1,13},{6,2},{10,6},{... | collective-permute-start | bytes 196616 | tf_op jit(solution)/shard_map/ppermute | solution.py:22
  23.3 0.7 copy-done.16
  24.3 0.8 gather_fusion.4
  25.3 2.3 %collective-permute-done = bf16[1,1,128,256]{3,1,2,0:T(2,128)(2,1)S(1)} collective-permute-done((bf16[1,1,128,256]{3,1,2,0:T(2,128)(2,1)S(1)}, bf16[1,1,128,256]{3,1,2,0:T(2,128)(2,1)S(1)}, u32[]{:S(2)}, u32[]{:S(2)}) %collective-permute-start) | collective-permute-done | bytes 65568 | tf_op jit(solution)/shard_map/ppermute | solution.py:20
  28.1 0.9 copy-done.13
  29.2 0.8 gather_fusion
  30.2 1.1 gather_fusion.5
  31.3 1.1 gather_fusion.1
  33.2 3.3 %collective-permute-start.9 = (bf16[1,4,21,256]{3,2,1,0:T(8,128)(2,1)S(1)}, bf16[1,4,21,256]{3,2,1,0:T(8,128)(2,1)S(1)}, u32[]{:S(2)}, u32[]{:S(2)}) collective-permute-start(bf16[1,4,21,256]{3,2,1,0:T(8,128)(2,1)S(1)} %get-tuple-element.28), channel_id=1, source_target_pairs={{4,0},{8,4},{12,8},{0,12},{5,1},{9,5},{13,9},{1,13},{6,2},{10,6},{... | collective-permute-start | bytes 129032 | tf_op jit(solution)/shard_map/ppermute | solution.py:36
  36.7 3.8 %collective-permute-start.3 = (bf16[1,4,21,256]{3,2,1,0:T(8,128)(2,1)S(1)}, bf16[1,4,21,256]{3,2,1,0:T(8,128)(2,1)S(1)}, u32[]{:S(2)}, u32[]{:S(2)}) collective-permute-start(bf16[1,4,21,256]{3,2,1,0:T(8,128)(2,1)S(1)} %get-tuple-element.34), channel_id=1, source_target_pairs={{4,0},{8,4},{12,8},{0,12},{5,1},{9,5},{13,9},{1,13},{6,2},{10,6},{... | collective-permute-start | bytes 129032 | tf_op jit(solution)/shard_map/ppermute | solution.py:36
  40.6 0.8 copy-done.7
  42.7 0.8 copy-done.10
  44.0 0.7 copy-done.9
  45.0 0.9 reshape.620
  46.8 2.5 %fusion.73 = (f32[4,8,63]{2,1,0:T(8,128)S(1)}, f32[4,8,63,63]{2,3,1,0:T(8,128)}) fusion(pred[4,63]{1,0:T(4,128)(4,1)S(1)} %gt.32, bf16[4,63,8,32]{1,0,3,2:T(4,128)(2,1)S(1)} %reshape.621, bf16[4,63,8,32]{1,0,3,2:T(4,128)(2,1)} %reshape.620), kind=kOutput, calls=%fused_computation.171 | convolution fusion | flops 8636606 | bytes 774396 | tf_op jit(solution)/shard_map/sub | solution.py:60
  49.3 2.8 %fusion.10 = bf16[4,63,8,32]{1,3,2,0:T(8,128)(2,1)} fusion(f32[4,8,63,63]{2,3,1,0:T(8,128)S(1)} %fusion.31, bf16[4,63,8,32]{1,0,3,2:T(4,128)(2,1)S(1)} %reshape.621, f32[4,8,63,63]{2,3,1,0:T(8,128)} %get-tuple-element.52, f32[4,8,63]{2,1,0:T(8,128)S(1)} %get-tuple-element.51), kind=kOutput, calls=%fused_computation.23 | convolution fusion | flops 9084158 | bytes 1282176 | tf_op jit(solution)/shard_map/jnqk,jknd->jqnd/dot_general | solution.py:95
  52.1 2.9 %fusion.11 = bf16[4,63,8,32]{1,3,2,0:T(8,128)(2,1)} fusion(f32[4,8,63,63]{2,3,1,0:T(8,128)S(1)} %fusion.31, bf16[4,63,8,32]{1,0,3,2:T(4,128)(2,1)} %reshape.620, f32[4,8,63,63]{2,3,1,0:T(8,128)} %get-tuple-element.52, f32[4,8,63]{2,1,0:T(8,128)S(1)} %get-tuple-element.51), kind=kOutput, calls=%fused_computation.24 | convolution fusion | flops 9084158 | bytes 1282176 | tf_op jit(solution)/shard_map/jnqk,jqnd->jknd/dot_general | solution.py:98
  54.9 1.7 fusion.12
  57.3 0.9 fusion.83
  58.5 0.7 copy-done.12
  59.6 0.9 fusion.80
  60.7 0.7 copy-done.11
  62.4 3.9 %collective-permute-start.7 = (bf16[1,4,21,256]{3,2,1,0:T(8,128)(2,1)S(1)}, bf16[1,4,21,256]{3,2,1,0:T(8,128)(2,1)S(1)}, u32[]{:S(2)}, u32[]{:S(2)}) collective-permute-start(bf16[1,4,21,256]{3,2,1,0:T(8,128)(2,1)S(1)} %get-tuple-element.31), channel_id=1, source_target_pairs={{4,0},{8,4},{12,8},{0,12},{5,1},{9,5},{13,9},{1,13},{6,2},{10,6},{... | collective-permute-start | bytes 129032 | tf_op jit(solution)/shard_map/ppermute | solution.py:36
  66.3 0.9 fusion.82
  67.2 0.9 fusion.81
  68.7 3.8 %collective-permute-start.11 = (bf16[1,4,21,256]{3,2,1,0:T(8,128)(2,1)S(1)}, bf16[1,4,21,256]{3,2,1,0:T(8,128)(2,1)S(1)}, u32[]{:S(2)}, u32[]{:S(2)}) collective-permute-start(bf16[1,4,21,256]{3,2,1,0:T(8,128)(2,1)S(1)} %get-tuple-element.25), channel_id=1, source_target_pairs={{4,0},{8,4},{12,8},{0,12},{5,1},{9,5},{13,9},{1,13},{6,2},{10,6},{... | collective-permute-start | bytes 129032 | tf_op jit(solution)/shard_map/ppermute | solution.py:36
  72.6 2.0 %collective-permute-done.10 = bf16[1,4,21,256]{3,2,1,0:T(8,128)(2,1)S(1)} collective-permute-done((bf16[1,4,21,256]{3,2,1,0:T(8,128)(2,1)S(1)}, bf16[1,4,21,256]{3,2,1,0:T(8,128)(2,1)S(1)}, u32[]{:S(2)}, u32[]{:S(2)}) %collective-permute-start.10) | collective-permute-done | bytes 43040 | tf_op jit(solution)/shard_map/ppermute | solution.py:36
  74.7 0.8 gather_fusion.2
  75.6 0.8 gather_fusion.6
  76.5 1.2 gather_fusion.7
  77.8 0.9 fusion.79
  79.0 1.2 gather_fusion.3
  80.7 3.9 %collective-permute-start.13 = (bf16[1,1,128,256]{3,2,1,0:T(8,128)(2,1)S(1)}, bf16[1,1,128,256]{3,2,1,0:T(8,128)(2,1)S(1)}, u32[]{:S(2)}, u32[]{:S(2)}) collective-permute-start(bf16[1,1,128,256]{3,2,1,0:T(8,128)(2,1)S(1)} %get-tuple-element.23), channel_id=1, source_target_pairs={{4,0},{8,4},{12,8},{0,12},{5,1},{9,5},{13,9},{1,13},{6,2},{10,6},{... | collective-permute-start | bytes 196616 | tf_op jit(solution)/shard_map/ppermute | solution.py:36
  84.6 0.8 add_convert_fusion.1
  85.3 1.4 collective-permute-done.12
  86.8 0.7 add_convert_fusion
  87.5 89.5 %all-reduce.9.cloned.1.call-done = (f32[256,256]{1,0:T(8,128)}, f32[256,256]{1,0:T(8,128)}, f32[256,256]{1,0:T(8,128)}, f32[256,256]{1,0:T(8,128)}, f32[256,256]{1,0:T(8,128)}) async-done(((f32[256,256]{1,0:T(8,128)}, f32[256,256]{1,0:T(8,128)}, f32[256,256]{1,0:T(8,128)}, f32[256,256]{1,0:T(8,128)}, f32[256,256]{1,0:T(8,128)}), (f32[256,256]{1,0:T(8,128)}, f32[256,256]{1,0:T(8,128)}, f32[256,256]{1,0:T(8,128)}, ...) | async-done | bytes 1310736 | tf_op jit(solution)/shard_map/psum | solution.py:279
  177.0 1.7 multiply_reduce_fusion.1
  180.1 0.7 multiply_reduce_fusion.4
  184.7 0.7 broadcast_multiply_fusion.3
  185.4 0.7 broadcast_multiply_fusion.2
  186.2 0.7 broadcast_multiply_fusion.1
  187.2 0.7 broadcast_multiply_fusion
  187.9 0.7 broadcast_multiply_fusion.4
  (132 shorter events, 12.8 us)
Async XLA Ops:
  7.2 21.0 %copy-start = (bf16[256,256]{1,0:T(8,128)(2,1)S(1)}, bf16[256,256]{1,0:T(8,128)(2,1)}, u32[]{:S(2)}) copy-start(bf16[256,256]{1,0:T(8,128)(2,1)} %param.23) | copy-start | bytes 393220
  7.2 169.8 %all-reduce.9.cloned.1.call-start = ((), (), s32[]{:S(2)}) async-start(), calls=%async_computation | async-start | bytes 2621440 | tf_op jit(solution)/shard_map/psum | solution.py:279
  7.2 0.7 copy-start.14
  12.9 12.2 %collective-permute-start.4 = (bf16[1,4,21]{2,1,0:T(4,128)(2,1)S(1)}, bf16[1,4,21]{2,1,0:T(4,128)(2,1)S(1)}, u32[]{:S(2)}, u32[]{:S(2)}) collective-permute-start(bf16[1,4,21]{2,1,0:T(4,128)(2,1)S(1)} %get-tuple-element.38), channel_id=1, source_target_pairs={{12,0},{0,4},{4,8},{8,12},{13,1},{1,5},{5,9},{9,13},{14,2},{2,6},{... | collective-permute-start | bytes 512 | tf_op jit(solution)/shard_map/ppermute | solution.py:36
  16.0 9.2 %collective-permute-start.5 = (bf16[1,4,21]{2,1,0:T(4,128)(2,1)S(1)}, bf16[1,4,21]{2,1,0:T(4,128)(2,1)S(1)}, u32[]{:S(2)}, u32[]{:S(2)}) collective-permute-start(bf16[1,4,21]{2,1,0:T(4,128)(2,1)S(1)} %get-tuple-element.39), channel_id=1, source_target_pairs={{4,0},{8,4},{12,8},{0,12},{5,1},{9,5},{13,9},{1,13},{6,2},{10,6},{... | collective-permute-start | bytes 512 | tf_op jit(solution)/shard_map/ppermute | solution.py:36
  19.1 5.2 %copy-start.1 = (bf16[1,256,256]{2,1,0:T(8,128)(2,1)S(1)}, bf16[1,256,256]{2,1,0:T(8,128)(2,1)}, u32[]{:S(2)}) copy-start(bf16[1,256,256]{2,1,0:T(8,128)(2,1)} %param.22) | copy-start | bytes 393220
  19.3 3.9 %copy-start.15 = (s32[1,128]{1,0:T(1,128)S(1)}, s32[1,128]{1,0:T(1,128)}, u32[]{:S(2)}) copy-start(s32[1,128]{1,0:T(1,128)} %param.20) | copy-start | bytes 1540
  19.3 8.2 %collective-permute-start = (bf16[1,1,128,256]{3,1,2,0:T(2,128)(2,1)S(1)}, bf16[1,1,128,256]{3,1,2,0:T(2,128)(2,1)S(1)}, u32[]{:S(2)}, u32[]{:S(2)}) collective-permute-start(bf16[1,1,128,256]{3,1,2,0:T(2,128)(2,1)S(1)} %get-tuple-element.36), channel_id=1, source_target_pairs={{0,4},{4,8},{8,12},{12,0},{1,5},{5,9},{9,13},{13,1},{2,6},{6,10},{... | collective-permute-start | bytes 196616 | tf_op jit(solution)/shard_map/ppermute | solution.py:20
  19.4 8.1 %collective-permute-start.1 = (bf16[1,1,128,256]{3,1,2,0:T(2,128)(2,1)S(1)}, bf16[1,1,128,256]{3,1,2,0:T(2,128)(2,1)S(1)}, u32[]{:S(2)}, u32[]{:S(2)}) collective-permute-start(bf16[1,1,128,256]{3,1,2,0:T(2,128)(2,1)S(1)} %get-tuple-element.37), channel_id=1, source_target_pairs={{4,0},{8,4},{12,8},{0,12},{5,1},{9,5},{13,9},{1,13},{6,2},{10,6},{... | collective-permute-start | bytes 196616 | tf_op jit(solution)/shard_map/ppermute | solution.py:22
  23.3 0.7 copy-start.16
  28.1 0.9 copy-start.13
  32.7 7.8 %collective-permute-start.8 = (bf16[1,4,21,256]{3,2,1,0:T(8,128)(2,1)S(1)}, bf16[1,4,21,256]{3,2,1,0:T(8,128)(2,1)S(1)}, u32[]{:S(2)}, u32[]{:S(2)}) collective-permute-start(bf16[1,4,21,256]{3,2,1,0:T(8,128)(2,1)S(1)} %get-tuple-element.27), channel_id=1, source_target_pairs={{12,0},{0,4},{4,8},{8,12},{13,1},{1,5},{5,9},{9,13},{14,2},{2,6},{... | collective-permute-start | bytes 129032 | tf_op jit(solution)/shard_map/ppermute | solution.py:36
  33.2 7.3 %collective-permute-start.9 = (bf16[1,4,21,256]{3,2,1,0:T(8,128)(2,1)S(1)}, bf16[1,4,21,256]{3,2,1,0:T(8,128)(2,1)S(1)}, u32[]{:S(2)}, u32[]{:S(2)}) collective-permute-start(bf16[1,4,21,256]{3,2,1,0:T(8,128)(2,1)S(1)} %get-tuple-element.28), channel_id=1, source_target_pairs={{4,0},{8,4},{12,8},{0,12},{5,1},{9,5},{13,9},{1,13},{6,2},{10,6},{... | collective-permute-start | bytes 129032 | tf_op jit(solution)/shard_map/ppermute | solution.py:36
  36.6 5.9 %collective-permute-start.2 = (bf16[1,4,21,256]{3,2,1,0:T(8,128)(2,1)S(1)}, bf16[1,4,21,256]{3,2,1,0:T(8,128)(2,1)S(1)}, u32[]{:S(2)}, u32[]{:S(2)}) collective-permute-start(bf16[1,4,21,256]{3,2,1,0:T(8,128)(2,1)S(1)} %get-tuple-element.33), channel_id=1, source_target_pairs={{12,0},{0,4},{4,8},{8,12},{13,1},{1,5},{5,9},{9,13},{14,2},{2,6},{... | collective-permute-start | bytes 129032 | tf_op jit(solution)/shard_map/ppermute | solution.py:36
  36.7 5.9 %collective-permute-start.3 = (bf16[1,4,21,256]{3,2,1,0:T(8,128)(2,1)S(1)}, bf16[1,4,21,256]{3,2,1,0:T(8,128)(2,1)S(1)}, u32[]{:S(2)}, u32[]{:S(2)}) collective-permute-start(bf16[1,4,21,256]{3,2,1,0:T(8,128)(2,1)S(1)} %get-tuple-element.34), channel_id=1, source_target_pairs={{4,0},{8,4},{12,8},{0,12},{5,1},{9,5},{13,9},{1,13},{6,2},{10,6},{... | collective-permute-start | bytes 129032 | tf_op jit(solution)/shard_map/ppermute | solution.py:36
  40.6 0.9 copy-start.7
  42.6 0.9 copy-start.10
  43.8 0.9 copy-start.9
  45.0 0.9 copy-start.8
  54.9 1.7 copy-start.17
  58.2 0.9 copy-start.12
  60.5 0.9 copy-start.11
  62.3 10.2 %collective-permute-start.6 = (bf16[1,4,21,256]{3,2,1,0:T(8,128)(2,1)S(1)}, bf16[1,4,21,256]{3,2,1,0:T(8,128)(2,1)S(1)}, u32[]{:S(2)}, u32[]{:S(2)}) collective-permute-start(bf16[1,4,21,256]{3,2,1,0:T(8,128)(2,1)S(1)} %get-tuple-element.30), channel_id=1, source_target_pairs={{12,0},{0,4},{4,8},{8,12},{13,1},{1,5},{5,9},{9,13},{14,2},{2,6},{... | collective-permute-start | bytes 129032 | tf_op jit(solution)/shard_map/ppermute | solution.py:36
  62.4 10.2 %collective-permute-start.7 = (bf16[1,4,21,256]{3,2,1,0:T(8,128)(2,1)S(1)}, bf16[1,4,21,256]{3,2,1,0:T(8,128)(2,1)S(1)}, u32[]{:S(2)}, u32[]{:S(2)}) collective-permute-start(bf16[1,4,21,256]{3,2,1,0:T(8,128)(2,1)S(1)} %get-tuple-element.31), channel_id=1, source_target_pairs={{4,0},{8,4},{12,8},{0,12},{5,1},{9,5},{13,9},{1,13},{6,2},{10,6},{... | collective-permute-start | bytes 129032 | tf_op jit(solution)/shard_map/ppermute | solution.py:36
  68.7 5.9 %collective-permute-start.10 = (bf16[1,4,21,256]{3,2,1,0:T(8,128)(2,1)S(1)}, bf16[1,4,21,256]{3,2,1,0:T(8,128)(2,1)S(1)}, u32[]{:S(2)}, u32[]{:S(2)}) collective-permute-start(bf16[1,4,21,256]{3,2,1,0:T(8,128)(2,1)S(1)} %get-tuple-element.24), channel_id=1, source_target_pairs={{12,0},{0,4},{4,8},{8,12},{13,1},{1,5},{5,9},{9,13},{14,2},{2,6},{... | collective-permute-start | bytes 129032 | tf_op jit(solution)/shard_map/ppermute | solution.py:36
  68.7 5.9 %collective-permute-start.11 = (bf16[1,4,21,256]{3,2,1,0:T(8,128)(2,1)S(1)}, bf16[1,4,21,256]{3,2,1,0:T(8,128)(2,1)S(1)}, u32[]{:S(2)}, u32[]{:S(2)}) collective-permute-start(bf16[1,4,21,256]{3,2,1,0:T(8,128)(2,1)S(1)} %get-tuple-element.25), channel_id=1, source_target_pairs={{4,0},{8,4},{12,8},{0,12},{5,1},{9,5},{13,9},{1,13},{6,2},{10,6},{... | collective-permute-start | bytes 129032 | tf_op jit(solution)/shard_map/ppermute | solution.py:36
  80.6 6.1 %collective-permute-start.12 = (bf16[1,1,128,256]{3,2,1,0:T(8,128)(2,1)S(1)}, bf16[1,1,128,256]{3,2,1,0:T(8,128)(2,1)S(1)}, u32[]{:S(2)}, u32[]{:S(2)}) collective-permute-start(bf16[1,1,128,256]{3,2,1,0:T(8,128)(2,1)S(1)} %get-tuple-element.22), channel_id=1, source_target_pairs={{12,0},{0,4},{4,8},{8,12},{13,1},{1,5},{5,9},{9,13},{14,2},{2,6},{... | collective-permute-start | bytes 196616 | tf_op jit(solution)/shard_map/ppermute | solution.py:36
  80.7 6.1 %collective-permute-start.13 = (bf16[1,1,128,256]{3,2,1,0:T(8,128)(2,1)S(1)}, bf16[1,1,128,256]{3,2,1,0:T(8,128)(2,1)S(1)}, u32[]{:S(2)}, u32[]{:S(2)}) collective-permute-start(bf16[1,1,128,256]{3,2,1,0:T(8,128)(2,1)S(1)} %get-tuple-element.23), channel_id=1, source_target_pairs={{4,0},{8,4},{12,8},{0,12},{5,1},{9,5},{13,9},{1,13},{6,2},{10,6},{... | collective-permute-start | bytes 196616 | tf_op jit(solution)/shard_map/ppermute | solution.py:36
  177.0 1.7 copy-start.4
  177.0 2.4 %copy-start.5 = (f32[256,256]{1,0:T(8,128)S(1)}, f32[256,256]{1,0:T(8,128)}, u32[]{:S(2)}) copy-start(f32[256,256]{1,0:T(8,128)} %get-tuple-element.13) | copy-start | bytes 786436
  178.7 1.3 copy-start.6
  179.4 1.3 copy-start.2
  186.2 1.0 copy-start.3
Sparse Core Ops, SparseCore 0:
  80.7 96.2 all-reduce.8
where the time goes:
time: 196 us; the launch traced here: 195 us
  waiting for transfers between devices  95.9 us (49%)
  starting transfers between devices  28.6 us (15%)
  local copies, waits for them, and re-layouts  19.7 us (10%)
  matrix products  18.4 us (9%)
  between operations  18.1 us (9%)
  other arithmetic  15 us (8%)
    psum x1, waiting for transfers between devices, on_device(): lax.psum((message_term, weight_terms[0], weight_terms[1], weight_terms[2]...  89.5 us
    ppermute x12, starting transfers between devices, passed_along(): return lax.ppermute(block, axis, route)  24.7 us
    unnamed x36, local copies, waits for them, and re-layouts  6.42 us
    reduce_sum x1, other arithmetic, on_device(): jnp.sum(jnp.where(targets[..., None] == slot_ids, positions[None, :, None...  4.57 us
    reduce_sum x5, other arithmetic, on_device(): jnp.sum(matrix * matrix)  4.34 us
    ppermute x12, waiting for transfers between devices, passed_along(): return lax.ppermute(block, axis, route)  4.01 us
  transfers between devices with their start and end apart: 15, of which 5 were waited for; matrix products, arithmetic and copies ran while one was open for 4% of the time, Pallas kernels for 0%

commit v1 on v0

--- a/solution.py
+++ b/solution.py
@@ -277,8 +277,10 @@
     )
     grad_cells = summed.astype(jnp.bfloat16).reshape(events, per_device, channels)
     totals = lax.psum(
-        (message_term, weight_terms[0], weight_terms[1], weight_terms[2], weight_terms[3]),
-        ("phi", "ev"),
+        lax.psum(
+            (message_term, weight_terms[0], weight_terms[1], weight_terms[2], weight_terms[3]), "ev"
+        ),
+        "phi",
     )
     squares = jnp.sum(jnp.stack([jnp.sum(matrix * matrix) for matrix in totals]))
     bound = math.sqrt(5.0) * channels

time: 196 us -> 204 us (1.041)
  waiting for transfers between devices: 95.9 us -> 104 us
    psum x0 -> x1, waiting for transfers between devices: none -> 56.8 us  [on_device(): lax.psum(lax.psum((message_term, weight_terms[0], weight_terms[1], weight...]
    psum x1, waiting for transfers between devices: 89.5 us -> 40.2 us  [on_device(): lax.psum((message_term, weight_terms[0], weight_terms[1], weight_terms[2]...]
  transfers between devices with their start and end apart: 15 -> 16, of which waited for: 5 -> 6; matrix products, arithmetic and copies ran while one was open for 4% -> 4% of each run, Pallas kernels for 0% -> 0%
where the time goes in v1:
time: 204 us
  waiting for transfers between devices  104 us (51%)
  starting transfers between devices  28.5 us (14%)
  local copies, waits for them, and re-layouts  19.7 us (10%)
  matrix products  18.3 us (9%)
  between operations  18.1 us (9%)
  other arithmetic  15 us (7%)
    psum x1, waiting for transfers between devices, on_device(): lax.psum(lax.psum((message_term, weight_terms[0], weight_terms[1], weight...  56.8 us
    psum x1, waiting for transfers between devices, on_device(): lax.psum((message_term, weight_terms[0], weight_terms[1], weight_terms[2]...  40.2 us
    ppermute x12, starting transfers between devices, passed_along(): return lax.ppermute(block, axis, route)  24.6 us
    unnamed x36, local copies, waits for them, and re-layouts  6.42 us
    ppermute x12, waiting for transfers between devices, passed_along(): return lax.ppermute(block, axis, route)  4.67 us
    reduce_sum x1, other arithmetic, on_device(): jnp.sum(jnp.where(targets[..., None] == slot_ids, positions[None, :, None...  4.57 us
    reduce_sum x5, other arithmetic, on_device(): jnp.sum(matrix * matrix)  4.34 us
  transfers between devices with their start and end apart: 16, of which 6 were waited for; matrix products, arithmetic and copies ran while one was open for 4% of the time, Pallas kernels for 0%

profile of v1, /device:TPU:0, one launch (start us, length us, event | category | flops | bytes accessed | tf_op | source)
XLA Modules:
  0.0 203.6 jit_solution(10289179477389052972)
XLA Ops:
  8.2 4.6 %fusion.41 = s32[252]{0:T(256)S(1)} fusion(s32[128]{0:T(128)S(1)} %iota_add_fusion, s32[128]{0:T(128)S(1)} %get-tuple-element.47), kind=kLoop, calls=%fused_computation.93 | loop fusion | flops 96516 | bytes 2032 | tf_op jit(solution)/shard_map/reduce_sum | solution.py:180
  12.9 3.1 %collective-permute-start.4 = (bf16[1,4,21]{2,1,0:T(4,128)(2,1)S(1)}, bf16[1,4,21]{2,1,0:T(4,128)(2,1)S(1)}, u32[]{:S(2)}, u32[]{:S(2)}) collective-permute-start(bf16[1,4,21]{2,1,0:T(4,128)(2,1)S(1)} %get-tuple-element.43), channel_id=1, source_target_pairs={{12,0},{0,4},{4,8},{8,12},{13,1},{1,5},{5,9},{9,13},{14,2},{2,6},{... | collective-permute-start | bytes 512 | tf_op jit(solution)/shard_map/ppermute | solution.py:36
  16.0 2.1 %collective-permute-start.5 = (bf16[1,4,21]{2,1,0:T(4,128)(2,1)S(1)}, bf16[1,4,21]{2,1,0:T(4,128)(2,1)S(1)}, u32[]{:S(2)}, u32[]{:S(2)}) collective-permute-start(bf16[1,4,21]{2,1,0:T(4,128)(2,1)S(1)} %get-tuple-element.44), channel_id=1, source_target_pairs={{4,0},{8,4},{12,8},{0,12},{5,1},{9,5},{13,9},{1,13},{6,2},{10,6},{... | collective-permute-start | bytes 512 | tf_op jit(solution)/shard_map/ppermute | solution.py:36
  18.1 1.0 copy.103
  19.4 3.8 %collective-permute-start.1 = (bf16[1,1,128,256]{3,1,2,0:T(2,128)(2,1)S(1)}, bf16[1,1,128,256]{3,1,2,0:T(2,128)(2,1)S(1)}, u32[]{:S(2)}, u32[]{:S(2)}) collective-permute-start(bf16[1,1,128,256]{3,1,2,0:T(2,128)(2,1)S(1)} %get-tuple-element.42), channel_id=1, source_target_pairs={{4,0},{8,4},{12,8},{0,12},{5,1},{9,5},{13,9},{1,13},{6,2},{10,6},{... | collective-permute-start | bytes 196616 | tf_op jit(solution)/shard_map/ppermute | solution.py:22
  24.3 0.8 gather_fusion.4
  25.3 2.3 %collective-permute-done = bf16[1,1,128,256]{3,1,2,0:T(2,128)(2,1)S(1)} collective-permute-done((bf16[1,1,128,256]{3,1,2,0:T(2,128)(2,1)S(1)}, bf16[1,1,128,256]{3,1,2,0:T(2,128)(2,1)S(1)}, u32[]{:S(2)}, u32[]{:S(2)}) %collective-permute-start) | collective-permute-done | bytes 65568 | tf_op jit(solution)/shard_map/ppermute | solution.py:20
  28.1 0.9 copy-done.13
  29.2 0.8 gather_fusion
  30.2 1.1 gather_fusion.5
  31.3 1.1 gather_fusion.1
  33.2 3.3 %collective-permute-start.9 = (bf16[1,4,21,256]{3,2,1,0:T(8,128)(2,1)S(1)}, bf16[1,4,21,256]{3,2,1,0:T(8,128)(2,1)S(1)}, u32[]{:S(2)}, u32[]{:S(2)}) collective-permute-start(bf16[1,4,21,256]{3,2,1,0:T(8,128)(2,1)S(1)} %get-tuple-element.33), channel_id=1, source_target_pairs={{4,0},{8,4},{12,8},{0,12},{5,1},{9,5},{13,9},{1,13},{6,2},{10,6},{... | collective-permute-start | bytes 129032 | tf_op jit(solution)/shard_map/ppermute | solution.py:36
  36.7 3.8 %collective-permute-start.3 = (bf16[1,4,21,256]{3,2,1,0:T(8,128)(2,1)S(1)}, bf16[1,4,21,256]{3,2,1,0:T(8,128)(2,1)S(1)}, u32[]{:S(2)}, u32[]{:S(2)}) collective-permute-start(bf16[1,4,21,256]{3,2,1,0:T(8,128)(2,1)S(1)} %get-tuple-element.39), channel_id=1, source_target_pairs={{4,0},{8,4},{12,8},{0,12},{5,1},{9,5},{13,9},{1,13},{6,2},{10,6},{... | collective-permute-start | bytes 129032 | tf_op jit(solution)/shard_map/ppermute | solution.py:36
  40.6 0.8 copy-done.7
  42.7 0.8 copy-done.10
  44.0 0.7 copy-done.9
  45.0 0.9 reshape.620
  46.8 2.5 %fusion.73 = (f32[4,8,63]{2,1,0:T(8,128)S(1)}, f32[4,8,63,63]{2,3,1,0:T(8,128)}) fusion(pred[4,63]{1,0:T(4,128)(4,1)S(1)} %gt.32, bf16[4,63,8,32]{1,0,3,2:T(4,128)(2,1)S(1)} %reshape.621, bf16[4,63,8,32]{1,0,3,2:T(4,128)(2,1)} %reshape.620), kind=kOutput, calls=%fused_computation.171 | convolution fusion | flops 8636606 | bytes 774396 | tf_op jit(solution)/shard_map/sub | solution.py:60
  49.3 2.8 %fusion.10 = bf16[4,63,8,32]{1,3,2,0:T(8,128)(2,1)} fusion(f32[4,8,63,63]{2,3,1,0:T(8,128)S(1)} %fusion.31, bf16[4,63,8,32]{1,0,3,2:T(4,128)(2,1)S(1)} %reshape.621, f32[4,8,63,63]{2,3,1,0:T(8,128)} %get-tuple-element.57, f32[4,8,63]{2,1,0:T(8,128)S(1)} %get-tuple-element.56), kind=kOutput, calls=%fused_computation.23 | convolution fusion | flops 9084158 | bytes 1282176 | tf_op jit(solution)/shard_map/jnqk,jknd->jqnd/dot_general | solution.py:95
  52.1 2.9 %fusion.11 = bf16[4,63,8,32]{1,3,2,0:T(8,128)(2,1)} fusion(f32[4,8,63,63]{2,3,1,0:T(8,128)S(1)} %fusion.31, bf16[4,63,8,32]{1,0,3,2:T(4,128)(2,1)} %reshape.620, f32[4,8,63,63]{2,3,1,0:T(8,128)} %get-tuple-element.57, f32[4,8,63]{2,1,0:T(8,128)S(1)} %get-tuple-element.56), kind=kOutput, calls=%fused_computation.24 | convolution fusion | flops 9084158 | bytes 1282176 | tf_op jit(solution)/shard_map/jnqk,jqnd->jknd/dot_general | solution.py:98
  54.9 1.7 fusion.12
  57.3 0.9 fusion.83
  58.4 0.7 copy-done.12
  59.6 0.9 fusion.80
  60.7 0.7 copy-done.11
  62.4 3.9 %collective-permute-start.7 = (bf16[1,4,21,256]{3,2,1,0:T(8,128)(2,1)S(1)}, bf16[1,4,21,256]{3,2,1,0:T(8,128)(2,1)S(1)}, u32[]{:S(2)}, u32[]{:S(2)}) collective-permute-start(bf16[1,4,21,256]{3,2,1,0:T(8,128)(2,1)S(1)} %get-tuple-element.36), channel_id=1, source_target_pairs={{4,0},{8,4},{12,8},{0,12},{5,1},{9,5},{13,9},{1,13},{6,2},{10,6},{... | collective-permute-start | bytes 129032 | tf_op jit(solution)/shard_map/ppermute | solution.py:36
  66.2 0.9 fusion.82
  67.2 0.9 fusion.81
  68.7 3.8 %collective-permute-start.11 = (bf16[1,4,21,256]{3,2,1,0:T(8,128)(2,1)S(1)}, bf16[1,4,21,256]{3,2,1,0:T(8,128)(2,1)S(1)}, u32[]{:S(2)}, u32[]{:S(2)}) collective-permute-start(bf16[1,4,21,256]{3,2,1,0:T(8,128)(2,1)S(1)} %get-tuple-element.30), channel_id=1, source_target_pairs={{4,0},{8,4},{12,8},{0,12},{5,1},{9,5},{13,9},{1,13},{6,2},{10,6},{... | collective-permute-start | bytes 129032 | tf_op jit(solution)/shard_map/ppermute | solution.py:36
  72.6 2.0 collective-permute-done.10
  74.7 0.8 gather_fusion.2
  75.5 0.8 gather_fusion.6
  76.5 1.2 gather_fusion.7
  77.8 0.9 fusion.79
  78.8 1.2 gather_fusion.3
  80.0 40.2 %all-reduce.11.cloned.1.call-done = (f32[256,256]{1,0:T(8,128)}, f32[256,256]{1,0:T(8,128)}, f32[256,256]{1,0:T(8,128)}, f32[256,256]{1,0:T(8,128)}, f32[256,256]{1,0:T(8,128)}) async-done(((f32[256,256]{1,0:T(8,128)}, f32[256,256]{1,0:T(8,128)}, f32[256,256]{1,0:T(8,128)}, f32[256,256]{1,0:T(8,128)}, f32[256,256]{1,0:T(8,128)}), (f32[256,256]{1,0:T(8,128)}, f32[256,256]{1,0:T(8,128)}, ...) | async-done | bytes 1310736 | tf_op jit(solution)/shard_map/psum | solution.py:280
  120.9 1.5 collective-permute-start.12
  122.4 2.3 %collective-permute-start.13 = (bf16[1,1,128,256]{3,2,1,0:T(8,128)(2,1)S(1)}, bf16[1,1,128,256]{3,2,1,0:T(8,128)(2,1)S(1)}, u32[]{:S(2)}, u32[]{:S(2)}) collective-permute-start(bf16[1,1,128,256]{3,2,1,0:T(8,128)(2,1)S(1)} %get-tuple-element.28), channel_id=1, source_target_pairs={{4,0},{8,4},{12,8},{0,12},{5,1},{9,5},{13,9},{1,13},{6,2},{10,6},{... | collective-permute-start | bytes 196616 | tf_op jit(solution)/shard_map/ppermute | solution.py:36
  124.8 0.8 add_convert_fusion.1
  125.5 2.1 %collective-permute-done.12 = bf16[1,1,128,256]{3,2,1,0:T(8,128)(2,1)S(1)} collective-permute-done((bf16[1,1,128,256]{3,2,1,0:T(8,128)(2,1)S(1)}, bf16[1,1,128,256]{3,2,1,0:T(8,128)(2,1)S(1)}, u32[]{:S(2)}, u32[]{:S(2)}) %collective-permute-start.12) | collective-permute-done | bytes 65568 | tf_op jit(solution)/shard_map/ppermute | solution.py:36
  127.6 0.7 add_convert_fusion
  128.3 56.8 %all-reduce.13.cloned.1.call-done = (f32[256,256]{1,0:T(8,128)}, f32[256,256]{1,0:T(8,128)}, f32[256,256]{1,0:T(8,128)}, f32[256,256]{1,0:T(8,128)}, f32[256,256]{1,0:T(8,128)}) async-done(((f32[256,256]{1,0:T(8,128)}, f32[256,256]{1,0:T(8,128)}, f32[256,256]{1,0:T(8,128)}, f32[256,256]{1,0:T(8,128)}, f32[256,256]{1,0:T(8,128)}), (f32[256,256]{1,0:T(8,128)}, f32[256,256]{1,0:T(8,128)}, ...) | async-done | bytes 1310736 | tf_op jit(solution)/shard_map/psum | solution.py:279
  185.1 1.7 multiply_reduce_fusion.1
  192.8 0.7 broadcast_multiply_fusion.3
  193.5 0.7 broadcast_multiply_fusion.2
  194.2 0.7 broadcast_multiply_fusion.1
  195.3 0.7 broadcast_multiply_fusion
  196.0 0.7 broadcast_multiply_fusion.4
  (135 shorter events, 14.1 us)
Async XLA Ops:
  7.2 21.0 %copy-start = (bf16[256,256]{1,0:T(8,128)(2,1)S(1)}, bf16[256,256]{1,0:T(8,128)(2,1)}, u32[]{:S(2)}) copy-start(bf16[256,256]{1,0:T(8,128)(2,1)} %param.23) | copy-start | bytes 393220
  7.2 113.0 %all-reduce.11.cloned.1.call-start = ((), (), s32[]{:S(2)}) async-start(), calls=%async_computation | async-start | bytes 2621440 | tf_op jit(solution)/shard_map/psum | solution.py:280
  7.2 0.7 copy-start.14
  12.9 12.2 %collective-permute-start.4 = (bf16[1,4,21]{2,1,0:T(4,128)(2,1)S(1)}, bf16[1,4,21]{2,1,0:T(4,128)(2,1)S(1)}, u32[]{:S(2)}, u32[]{:S(2)}) collective-permute-start(bf16[1,4,21]{2,1,0:T(4,128)(2,1)S(1)} %get-tuple-element.43), channel_id=1, source_target_pairs={{12,0},{0,4},{4,8},{8,12},{13,1},{1,5},{5,9},{9,13},{14,2},{2,6},{... | collective-permute-start | bytes 512 | tf_op jit(solution)/shard_map/ppermute | solution.py:36
  16.0 9.2 %collective-permute-start.5 = (bf16[1,4,21]{2,1,0:T(4,128)(2,1)S(1)}, bf16[1,4,21]{2,1,0:T(4,128)(2,1)S(1)}, u32[]{:S(2)}, u32[]{:S(2)}) collective-permute-start(bf16[1,4,21]{2,1,0:T(4,128)(2,1)S(1)} %get-tuple-element.44), channel_id=1, source_target_pairs={{4,0},{8,4},{12,8},{0,12},{5,1},{9,5},{13,9},{1,13},{6,2},{10,6},{... | collective-permute-start | bytes 512 | tf_op jit(solution)/shard_map/ppermute | solution.py:36
  19.1 5.2 %copy-start.1 = (bf16[1,256,256]{2,1,0:T(8,128)(2,1)S(1)}, bf16[1,256,256]{2,1,0:T(8,128)(2,1)}, u32[]{:S(2)}) copy-start(bf16[1,256,256]{2,1,0:T(8,128)(2,1)} %param.22) | copy-start | bytes 393220
  19.3 3.9 %copy-start.15 = (s32[1,128]{1,0:T(1,128)S(1)}, s32[1,128]{1,0:T(1,128)}, u32[]{:S(2)}) copy-start(s32[1,128]{1,0:T(1,128)} %param.20) | copy-start | bytes 1540
  19.3 8.2 %collective-permute-start = (bf16[1,1,128,256]{3,1,2,0:T(2,128)(2,1)S(1)}, bf16[1,1,128,256]{3,1,2,0:T(2,128)(2,1)S(1)}, u32[]{:S(2)}, u32[]{:S(2)}) collective-permute-start(bf16[1,1,128,256]{3,1,2,0:T(2,128)(2,1)S(1)} %get-tuple-element.41), channel_id=1, source_target_pairs={{0,4},{4,8},{8,12},{12,0},{1,5},{5,9},{9,13},{13,1},{2,6},{6,10},{... | collective-permute-start | bytes 196616 | tf_op jit(solution)/shard_map/ppermute | solution.py:20
  19.4 8.1 %collective-permute-start.1 = (bf16[1,1,128,256]{3,1,2,0:T(2,128)(2,1)S(1)}, bf16[1,1,128,256]{3,1,2,0:T(2,128)(2,1)S(1)}, u32[]{:S(2)}, u32[]{:S(2)}) collective-permute-start(bf16[1,1,128,256]{3,1,2,0:T(2,128)(2,1)S(1)} %get-tuple-element.42), channel_id=1, source_target_pairs={{4,0},{8,4},{12,8},{0,12},{5,1},{9,5},{13,9},{1,13},{6,2},{10,6},{... | collective-permute-start | bytes 196616 | tf_op jit(solution)/shard_map/ppermute | solution.py:22
  23.3 0.7 copy-start.16
  28.1 0.9 copy-start.13
  32.7 7.8 %collective-permute-start.8 = (bf16[1,4,21,256]{3,2,1,0:T(8,128)(2,1)S(1)}, bf16[1,4,21,256]{3,2,1,0:T(8,128)(2,1)S(1)}, u32[]{:S(2)}, u32[]{:S(2)}) collective-permute-start(bf16[1,4,21,256]{3,2,1,0:T(8,128)(2,1)S(1)} %get-tuple-element.32), channel_id=1, source_target_pairs={{12,0},{0,4},{4,8},{8,12},{13,1},{1,5},{5,9},{9,13},{14,2},{2,6},{... | collective-permute-start | bytes 129032 | tf_op jit(solution)/shard_map/ppermute | solution.py:36
  33.2 7.3 %collective-permute-start.9 = (bf16[1,4,21,256]{3,2,1,0:T(8,128)(2,1)S(1)}, bf16[1,4,21,256]{3,2,1,0:T(8,128)(2,1)S(1)}, u32[]{:S(2)}, u32[]{:S(2)}) collective-permute-start(bf16[1,4,21,256]{3,2,1,0:T(8,128)(2,1)S(1)} %get-tuple-element.33), channel_id=1, source_target_pairs={{4,0},{8,4},{12,8},{0,12},{5,1},{9,5},{13,9},{1,13},{6,2},{10,6},{... | collective-permute-start | bytes 129032 | tf_op jit(solution)/shard_map/ppermute | solution.py:36
  36.6 5.9 %collective-permute-start.2 = (bf16[1,4,21,256]{3,2,1,0:T(8,128)(2,1)S(1)}, bf16[1,4,21,256]{3,2,1,0:T(8,128)(2,1)S(1)}, u32[]{:S(2)}, u32[]{:S(2)}) collective-permute-start(bf16[1,4,21,256]{3,2,1,0:T(8,128)(2,1)S(1)} %get-tuple-element.38), channel_id=1, source_target_pairs={{12,0},{0,4},{4,8},{8,12},{13,1},{1,5},{5,9},{9,13},{14,2},{2,6},{... | collective-permute-start | bytes 129032 | tf_op jit(solution)/shard_map/ppermute | solution.py:36
  36.7 5.9 %collective-permute-start.3 = (bf16[1,4,21,256]{3,2,1,0:T(8,128)(2,1)S(1)}, bf16[1,4,21,256]{3,2,1,0:T(8,128)(2,1)S(1)}, u32[]{:S(2)}, u32[]{:S(2)}) collective-permute-start(bf16[1,4,21,256]{3,2,1,0:T(8,128)(2,1)S(1)} %get-tuple-element.39), channel_id=1, source_target_pairs={{4,0},{8,4},{12,8},{0,12},{5,1},{9,5},{13,9},{1,13},{6,2},{10,6},{... | collective-permute-start | bytes 129032 | tf_op jit(solution)/shard_map/ppermute | solution.py:36
  40.6 0.9 copy-start.7
  42.6 0.9 copy-start.10
  43.8 0.9 copy-start.9
  45.0 0.9 copy-start.8
  54.9 1.7 copy-start.17
  58.2 0.9 copy-start.12
  60.5 0.9 copy-start.11
  62.3 10.2 %collective-permute-start.6 = (bf16[1,4,21,256]{3,2,1,0:T(8,128)(2,1)S(1)}, bf16[1,4,21,256]{3,2,1,0:T(8,128)(2,1)S(1)}, u32[]{:S(2)}, u32[]{:S(2)}) collective-permute-start(bf16[1,4,21,256]{3,2,1,0:T(8,128)(2,1)S(1)} %get-tuple-element.35), channel_id=1, source_target_pairs={{12,0},{0,4},{4,8},{8,12},{13,1},{1,5},{5,9},{9,13},{14,2},{2,6},{... | collective-permute-start | bytes 129032 | tf_op jit(solution)/shard_map/ppermute | solution.py:36
  62.4 10.2 %collective-permute-start.7 = (bf16[1,4,21,256]{3,2,1,0:T(8,128)(2,1)S(1)}, bf16[1,4,21,256]{3,2,1,0:T(8,128)(2,1)S(1)}, u32[]{:S(2)}, u32[]{:S(2)}) collective-permute-start(bf16[1,4,21,256]{3,2,1,0:T(8,128)(2,1)S(1)} %get-tuple-element.36), channel_id=1, source_target_pairs={{4,0},{8,4},{12,8},{0,12},{5,1},{9,5},{13,9},{1,13},{6,2},{10,6},{... | collective-permute-start | bytes 129032 | tf_op jit(solution)/shard_map/ppermute | solution.py:36
  68.6 5.9 %collective-permute-start.10 = (bf16[1,4,21,256]{3,2,1,0:T(8,128)(2,1)S(1)}, bf16[1,4,21,256]{3,2,1,0:T(8,128)(2,1)S(1)}, u32[]{:S(2)}, u32[]{:S(2)}) collective-permute-start(bf16[1,4,21,256]{3,2,1,0:T(8,128)(2,1)S(1)} %get-tuple-element.29), channel_id=1, source_target_pairs={{12,0},{0,4},{4,8},{8,12},{13,1},{1,5},{5,9},{9,13},{14,2},{2,6},{... | collective-permute-start | bytes 129032 | tf_op jit(solution)/shard_map/ppermute | solution.py:36
  68.7 5.9 %collective-permute-start.11 = (bf16[1,4,21,256]{3,2,1,0:T(8,128)(2,1)S(1)}, bf16[1,4,21,256]{3,2,1,0:T(8,128)(2,1)S(1)}, u32[]{:S(2)}, u32[]{:S(2)}) collective-permute-start(bf16[1,4,21,256]{3,2,1,0:T(8,128)(2,1)S(1)} %get-tuple-element.30), channel_id=1, source_target_pairs={{4,0},{8,4},{12,8},{0,12},{5,1},{9,5},{13,9},{1,13},{6,2},{10,6},{... | collective-permute-start | bytes 129032 | tf_op jit(solution)/shard_map/ppermute | solution.py:36
  78.7 106.4 %all-reduce.13.cloned.1.call-start = ((), (), s32[]{:S(2)}) async-start(), calls=%async_computation.1 | async-start | bytes 2621440 | tf_op jit(solution)/shard_map/psum | solution.py:279
  120.9 6.7 %collective-permute-start.12 = (bf16[1,1,128,256]{3,2,1,0:T(8,128)(2,1)S(1)}, bf16[1,1,128,256]{3,2,1,0:T(8,128)(2,1)S(1)}, u32[]{:S(2)}, u32[]{:S(2)}) collective-permute-start(bf16[1,1,128,256]{3,2,1,0:T(8,128)(2,1)S(1)} %get-tuple-element.27), channel_id=1, source_target_pairs={{12,0},{0,4},{4,8},{8,12},{13,1},{1,5},{5,9},{9,13},{14,2},{2,6},{... | collective-permute-start | bytes 196616 | tf_op jit(solution)/shard_map/ppermute | solution.py:36
  122.4 5.2 %collective-permute-start.13 = (bf16[1,1,128,256]{3,2,1,0:T(8,128)(2,1)S(1)}, bf16[1,1,128,256]{3,2,1,0:T(8,128)(2,1)S(1)}, u32[]{:S(2)}, u32[]{:S(2)}) collective-permute-start(bf16[1,1,128,256]{3,2,1,0:T(8,128)(2,1)S(1)} %get-tuple-element.28), channel_id=1, source_target_pairs={{4,0},{8,4},{12,8},{0,12},{5,1},{9,5},{13,9},{1,13},{6,2},{10,6},{... | collective-permute-start | bytes 196616 | tf_op jit(solution)/shard_map/ppermute | solution.py:36
  185.1 1.7 copy-start.4
  185.1 2.4 %copy-start.5 = (f32[256,256]{1,0:T(8,128)S(1)}, f32[256,256]{1,0:T(8,128)}, u32[]{:S(2)}) copy-start(f32[256,256]{1,0:T(8,128)} %get-tuple-element.18) | copy-start | bytes 786436
  186.8 1.3 copy-start.6
  187.5 1.3 copy-start.2
  194.2 1.0 copy-start.3
Sparse Core Ops, SparseCore 0:
  78.9 41.2 all-reduce.10
  122.9 62.1 all-reduce.12
